TPU v7x, 32 devices: a whole 2x2x4 slice. The times are simulated.
32 devices in a mesh: group: 2 (over y), tm: 4 (over z), seq: 2 (over x), mp: 2 (over core).
Axes of the slice: x: 2, y: 2, z: 4, core: 2. Of those that a mesh axis runs over, the one named last changes fastest.
Arguments:
- states: bfloat16 [8, 128, 5120], P(('group', 'tm'), 'seq'), parts along dimension 0, may hold values from -6 to 6
- start_step: int32 [2], P('group'), parts along dimension 0, may hold values from 0 to 96
- w_qkv: bfloat16 [3, 5120, 3072], P(None, 'tm', ('seq', 'mp')), may hold values from -0.078125 to 0.078125
- qk_gain: float32 [2, 3072], P(None, ('seq', 'mp')), may hold values from 0.25 to 1.75
- w_out: bfloat16 [5120, 3072], P('tm', ('seq', 'mp')), may hold values from -0.109375 to 0.109375
- time_proj: bfloat16 [256, 15360], P('tm'), may hold values from -0.375 to 0.375
Outputs:
- displacement: float32 [8, 128, 5120], P(('group', 'tm'), 'seq', 'mp'), parts along dimension 0
There are 2 independent parts, one for each index of `group`. A program takes and returns all parts, laid end to end along the dimension named above; an argument that names none is the same for every part. Nothing has to cross between parts.
Inputs may be any that keep to these rules, and one draw needn't show every extreme that they name: `start_step`: the window lies inside the trajectory.
All inputs are finite; a program needn't handle non-finite values.
Results may differ from a plain program's by a relative error of at most 0.0029.
Values may be sent and summed in bfloat16 or wider, within the bound.
No kernel may reach another device: no remote copies, remote signals or barrier semaphores. Data moves between devices by JAX's collectives and lax.ppermute only.
A program may use at most 128 MiB of HBM per device.

v0:
```python
import jax
import jax.numpy as jnp
from jax import lax
from jax.sharding import PartitionSpec as P

HEAD_DIM = 128
FREQ = 256
STEPS = 100
sample_shift = 5.0
norm_eps = 1e-06


def from_behind(block, axis, distance):
    devices = range(lax.axis_size(axis))
    route = [(i - distance, i) for i in devices if i - distance in devices]
    return lax.ppermute(block, axis, route)


def sigma_of(index):
    unit = 1.0 - index.astype(jnp.float32) / jnp.float32(STEPS)
    return sample_shift * unit / (1.0 + (sample_shift - 1.0) * unit)


def embed_time(sigma_now):
    half_freq = FREQ // 2
    ranks = jnp.arange(half_freq).astype(jnp.float32)
    freqs = jnp.exp(-jnp.log(jnp.float32(10000.0)) * ranks / jnp.float32(half_freq))
    angles = (1000.0 * sigma_now)[:, None] * freqs[None, :]
    return jnp.concatenate([jnp.cos(angles), jnp.sin(angles)], axis=1).astype(jnp.bfloat16)


def head_norm(values, gain, frames, seq_len, heads_dev):
    shaped = values.reshape(frames, seq_len, heads_dev, HEAD_DIM)
    meansq = jnp.mean(shaped * shaped, axis=-1, keepdims=True)
    scaled = shaped * lax.rsqrt(meansq + norm_eps) * gain.reshape(heads_dev, HEAD_DIM)
    return scaled.astype(jnp.bfloat16)


def attend(query, keys, values):
    frames, seq_len, heads_dev, head_size = query.shape
    block = min(seq_len, 512)
    blocks = seq_len // block
    inv_root = 1.0 / jnp.sqrt(jnp.float32(head_size))
    stacked = query.reshape(frames, blocks, block, heads_dev, head_size).transpose(1, 0, 2, 3, 4)

    def one_block(q_block):
        scores = (
            jnp.einsum("wqhd,wkhd->whqk", q_block, keys, preferred_element_type=jnp.float32)
            * inv_root
        )
        expo = jnp.exp(scores)
        probs = (expo / jnp.sum(expo, axis=-1, keepdims=True)).astype(jnp.bfloat16)
        return jnp.einsum(
            "whqk,wkhd->wqhd", probs, values, preferred_element_type=jnp.float32
        ).astype(jnp.bfloat16)

    result = lax.map(one_block, stacked)
    return result.transpose(1, 0, 2, 3, 4).reshape(frames, seq_len, heads_dev * head_size)


def on_device(states, start_step, w_qkv, qk_gain, w_out, time_proj):
    frames, tok, width = states.shape
    n_tm = lax.axis_size("tm")
    n_mp = lax.axis_size("mp")
    window = frames * n_tm
    tm_pos = lax.axis_index("tm")
    steps_idx = start_step[0] + jnp.arange(window)
    sigma_now = sigma_of(steps_idx)
    step_size = sigma_of(steps_idx + 1) - sigma_now
    emb = embed_time(sigma_now)
    freq_rows = time_proj.shape[0]
    emb_cols = lax.dynamic_slice_in_dim(emb, tm_pos * freq_rows, freq_rows, 1)
    modulation = lax.psum_scatter(
        jnp.dot(emb_cols, time_proj, preferred_element_type=jnp.float32),
        "tm",
        scatter_dimension=0,
        tiled=True,
    )
    shift = modulation[:, :width]
    scale = modulation[:, width : 2 * width]
    gate = modulation[:, 2 * width :]
    field = states.astype(jnp.float32)
    mean = jnp.mean(field, axis=-1, keepdims=True)
    centred = field - mean
    var = jnp.mean(centred * centred, axis=-1, keepdims=True)
    normed = centred * lax.rsqrt(var + norm_eps)
    hidden = (normed * (1.0 + scale[:, None, :]) + shift[:, None, :]).astype(jnp.bfloat16)
    whole = lax.all_gather(hidden, "seq", axis=1, tiled=True)
    seq_len = whole.shape[1]
    flat = whole.reshape(frames * seq_len, width)
    head_cols = w_qkv.shape[2]
    heads_dev = head_cols // HEAD_DIM
    proj = jnp.einsum(
        "rd,cdh->crh",
        flat,
        lax.all_gather(w_qkv, "tm", axis=1, tiled=True),
        preferred_element_type=jnp.float32,
    )
    query = head_norm(proj[0], qk_gain[0], frames, seq_len, heads_dev)
    keys = head_norm(proj[1], qk_gain[1], frames, seq_len, heads_dev)
    values = proj[2].astype(jnp.bfloat16).reshape(frames, seq_len, heads_dev, HEAD_DIM)
    attn = attend(query, keys, values)
    out_full = lax.all_gather(w_out, "tm", axis=0, tiled=True)
    half_width = width // n_mp
    rows = frames * tok
    first = jnp.int32(0) // rows
    pieces = []
    for offset in range(rows * lax.axis_size(("seq", "mp")) // rows):
        owner = first + offset
        segment = owner // n_mp
        column = owner % n_mp
        tokens_part = lax.dynamic_slice_in_dim(attn, segment * tok, tok, 1)
        weight_part = lax.dynamic_slice_in_dim(out_full, column * half_width, half_width, 0)
        product = jnp.einsum(
            "tsh,eh->tse", tokens_part, weight_part, preferred_element_type=jnp.float32
        )
        pieces.append(product.reshape(rows, half_width))
    out_part = lax.psum_scatter(
        jnp.concatenate(pieces, axis=0), ("seq", "mp"), scatter_dimension=0, tiled=True
    ).reshape(frames, tok, half_width)
    gate_own = lax.dynamic_slice_in_dim(gate, lax.axis_index("mp") * half_width, half_width, 1)
    own_steps = lax.dynamic_slice_in_dim(step_size, tm_pos * frames, frames, 0)
    drift = gate_own[:, None, :] * out_part
    increments = own_steps[:, None, None] * drift
    local_sums = jnp.cumsum(increments, axis=0)
    block_total = local_sums[-1]
    running = block_total
    for level in range((n_tm - 1).bit_length()):
        running = running + from_behind(running, "tm", 1 << level)
    before = running - block_total
    return before[None, :, :] + local_sums


def solution(mesh):
    return jax.shard_map(
        on_device,
        mesh=mesh,
        in_specs=(
            P(("group", "tm"), "seq", None),
            P("group"),
            P(None, "tm", ("seq", "mp")),
            P(None, ("seq", "mp")),
            P("tm", ("seq", "mp")),
            P("tm", None),
        ),
        out_specs=P(("group", "tm"), "seq", "mp"),
        check_vma=False,
    )
```

profile of v0, /device:TPU:25, one launch (start us, length us, event | category | flops | bytes accessed | tf_op | source)
XLA Modules:
  0.0 721.7 jit_solution(13477119722304982495)
XLA Ops:
  8.3 1.1 fusion.26
  10.7 32.4 %all-reduce.3.cloned.1.call-done = f32[4,15360]{1,0:T(4,128)} async-done(((f32[4,15360]{1,0:T(4,128)}), f32[4,15360]{1,0:T(4,128)}) %all-reduce.3.cloned.1.call-update) | async-done | bytes 245776
  43.0 1.7 dynamic-slice_add_fusion
  44.7 1.1 fusion.13
  47.3 25.9 %all-gather.4.cloned.1.call-done = bf16[1,128,5120]{2,1,0:T(8,128)(2,1)} async-done(((bf16[1,64,5120]{2,1,0:T(8,128)(2,1)}), bf16[1,128,5120]{2,1,0:T(8,128)(2,1)}) %all-gather.4.cloned.1.call-update) | async-done | bytes 1310736 | tf_op jit(solution)/shard_map/all_gather | solution.py:88
  73.2 398.3 %all-gather.6.cloned.1.call-done = bf16[3,5120,768]{2,1,0:T(8,128)(2,1)} async-done(((bf16[3,1280,768]{2,1,0:T(8,128)(2,1)}), bf16[3,5120,768]{2,1,0:T(8,128)(2,1)}) %all-gather.6.cloned.1.call-update) | async-done | bytes 23592976 | tf_op jit(solution)/shard_map/all_gather | solution.py:96
  471.4 10.0 %convolution_bitcast_fusion = f32[3,128,768]{2,1,0:T(8,128)S(1)} fusion(bf16[3,5120,768]{2,1,0:T(8,128)(2,1)} %all-gather.6.cloned.1.call-done, bf16[1,128,5120]{2,1,0:T(8,128)(2,1)} %all-gather.4.cloned.1.call-done), kind=kOutput, calls=%fused_computation.13 | convolution fusion | flops 3019898880 | bytes 26083328 | tf_op jit(solution)/shard_map/rd,cdh->crh/dot_general | solution.py:93
  483.3 1.1 reduce_sum.49
  484.8 1.1 copy.19
  486.7 125.4 %all-gather.8.cloned.1.call-done = bf16[5120,768]{1,0:T(8,128)(2,1)} async-done(((bf16[1280,768]{1,0:T(8,128)(2,1)}), bf16[5120,768]{1,0:T(8,128)(2,1)}) %all-gather.8.cloned.1.call-update) | async-done | bytes 7864336 | tf_op jit(solution)/shard_map/all_gather | solution.py:103
  612.1 3.6 fusion.2
  615.7 3.6 fusion.4
  619.3 1.3 fusion.6
  620.6 1.5 fusion
  622.1 1.7 pad_maximum_fusion
  624.9 1.5 dynamic-slice_reduce_fusion
  626.4 32.9 %reduce-scatter.2.cloned.1.call-done = f32[64,2560]{1,0:T(8,128)} async-done(((f32[256,2560]{1,0:T(8,128)}), f32[64,2560]{1,0:T(8,128)}) %reduce-scatter.2.cloned.1.call-update) | async-done | bytes 655376 | tf_op jit(solution)/shard_map/reduce_scatter | solution.py:118
  659.4 1.8 multiply_multiply_fusion
  661.1 1.3 collective-permute-start
  662.4 16.1 %collective-permute-done = f32[64,2560]{1,0:T(8,128)S(1)} collective-permute-done((f32[64,2560]{1,0:T(8,128)S(1)}, f32[64,2560]{1,0:T(8,128)S(1)}, u32[]{:S(2)}, u32[]{:S(2)}) %collective-permute-start) | collective-permute-done | bytes 655392 | tf_op jit(solution)/shard_map/ppermute | solution.py:16
  678.5 1.7 fusion.35
  680.2 1.3 collective-permute-start.1
  681.5 32.1 %collective-permute-done.1 = f32[64,2560]{1,0:T(8,128)S(1)} collective-permute-done((f32[64,2560]{1,0:T(8,128)S(1)}, f32[64,2560]{1,0:T(8,128)S(1)}, u32[]{:S(2)}, u32[]{:S(2)}) %collective-permute-start.1) | collective-permute-done | bytes 655392 | tf_op jit(solution)/shard_map/ppermute | solution.py:16
  713.7 1.5 fusion.16
  (45 shorter events, 7.7 us)
Async XLA Ops:
  6.5 1.8 copy-start
  6.5 3.5 copy-start.6
  6.5 3.0 copy-start.2
  6.5 36.5 %all-reduce.3.cloned.1.call-start = ((), (), s32[]{:S(2)}) async-start(), calls=%async_computation.5 | async-start | bytes 491520
  9.5 63.7 %all-gather.4.cloned.1.call-start = ((), (), s32[]{:S(2)}) async-start(), calls=%async_computation.1 | async-start | bytes 1966080 | tf_op jit(solution)/shard_map/all_gather | solution.py:88
  45.9 1.4 copy-start.4
  45.9 425.6 %all-gather.6.cloned.1.call-start = ((), (), s32[]{:S(2)}) async-start(), calls=%async_computation.2 | async-start | bytes 29491200 | tf_op jit(solution)/shard_map/all_gather | solution.py:96
  46.6 565.5 %all-gather.8.cloned.1.call-start = ((), (), s32[]{:S(2)}) async-start(), calls=%async_computation.3 | async-start | bytes 9830400 | tf_op jit(solution)/shard_map/all_gather | solution.py:103
  47.2 612.2 %reduce-scatter.2.cloned.1.call-start = ((), (), s32[]{:S(2)}) async-start(), calls=%async_computation.4 | async-start | bytes 3276800 | tf_op jit(solution)/shard_map/reduce_scatter | solution.py:118
  612.1 7.1 copy-start.1
  623.8 0.6 copy-start.5
  659.4 54.3 %copy-start.3 = (f32[64,2560]{1,0:T(8,128)S(1)}, f32[64,2560]{1,0:T(8,128)}, u32[]{:S(2)}) copy-start(f32[64,2560]{1,0:T(8,128)} %reduce-scatter.2.cloned.1.call-done) | copy-start | bytes 1966084
  661.1 17.4 %collective-permute-start = (f32[64,2560]{1,0:T(8,128)S(1)}, f32[64,2560]{1,0:T(8,128)S(1)}, u32[]{:S(2)}, u32[]{:S(2)}) collective-permute-start(f32[64,2560]{1,0:T(8,128)S(1)} %multiply_multiply_fusion), channel_id=1, source_target_pairs={{0,4},{4,8},{8,12},{1,5},{5,9},{9,13},{2,6},{6,10},{10,14},{3,7},{... | collective-permute-start | bytes 1966088 | tf_op jit(solution)/shard_map/ppermute | solution.py:16
  680.2 33.4 %collective-permute-start.1 = (f32[64,2560]{1,0:T(8,128)S(1)}, f32[64,2560]{1,0:T(8,128)S(1)}, u32[]{:S(2)}, u32[]{:S(2)}) collective-permute-start(f32[64,2560]{1,0:T(8,128)S(1)} %fusion.35), channel_id=1, source_target_pairs={{0,8},{4,12},{1,9},{5,13},{2,10},{6,14},{3,11},{7,15},{16,24},{20,... | collective-permute-start | bytes 1966088 | tf_op jit(solution)/shard_map/ppermute | solution.py:16
Sparse Core Ops, SparseCore 0:
  9.7 33.3 all-reduce.2
  46.0 27.1 all-gather.3
  74.7 396.6 all-gather.5
  472.9 139.2 all-gather.7
  623.9 35.4 reduce-scatter.1
where the time goes:
time: 722 us
  waiting for transfers between devices  664 us (92%)
  matrix products  21.8 us (3%)
  between operations  14.1 us (2%)
  other arithmetic  12 us (2%)
    all_gather x1, waiting for transfers between devices, on_device(): lax.all_gather(w_qkv, 'tm', axis=1, tiled=True)  398 us
    all_gather x1, waiting for transfers between devices, on_device(): out_full = lax.all_gather(w_out, 'tm', axis=0, tiled=True)  125 us
    ppermute x2, waiting for transfers between devices, from_behind(): return lax.ppermute(block, axis, route)  48.2 us
    unnamed x6, waiting for transfers between devices  33.6 us
    reduce_scatter x1, waiting for transfers between devices, on_device(): lax.psum_scatter(jnp.concatenate(pieces, axis=0), ('seq', 'mp'), scatter_...  32.9 us
    all_gather x1, waiting for transfers between devices, on_device(): whole = lax.all_gather(hidden, 'seq', axis=1, tiled=True)  25.9 us
  transfers between devices with their start and end apart: 7, of which 7 were waited for; matrix products, arithmetic and copies ran while one was open for 3% of the time, Pallas kernels for 0%

commit v1 on v0

--- a/solution.py
+++ b/solution.py
@@ -8,6 +8,22 @@
 STEPS = 100
 sample_shift = 5.0
 norm_eps = 1e-06
+
+
+def summed_both_ways(shard, axis, dim, product):
+    peers, index, rows = (lax.axis_size(axis), lax.axis_index(axis), shard.shape[dim])
+    ahead = [(i, (i + 1) % peers) for i in range(peers)]
+    behind = [(i, (i - 1) % peers) for i in range(peers)]
+    half = peers // 2
+    from_left = from_right = shard
+    total = product(shard, index * rows)
+    for hop in range(1, half + 1):
+        from_left = lax.ppermute(from_left, axis, ahead)
+        if hop < peers - half:
+            from_right = lax.ppermute(from_right, axis, behind)
+            total = total + product(from_right, (index + hop) % peers * rows)
+        total = total + product(from_left, (index - hop) % peers * rows)
+    return total
 
 
 def from_behind(block, axis, distance):
@@ -90,11 +106,16 @@
     flat = whole.reshape(frames * seq_len, width)
     head_cols = w_qkv.shape[2]
     heads_dev = head_cols // HEAD_DIM
-    proj = jnp.einsum(
-        "rd,cdh->crh",
-        flat,
-        lax.all_gather(w_qkv, "tm", axis=1, tiled=True),
-        preferred_element_type=jnp.float32,
+    proj = summed_both_ways(
+        w_qkv,
+        "tm",
+        1,
+        lambda shard, at: jnp.einsum(
+            "rd,cdh->crh",
+            lax.dynamic_slice_in_dim(flat, at, shard.shape[1], axis=1),
+            shard,
+            preferred_element_type=jnp.float32,
+        ),
     )
     query = head_norm(proj[0], qk_gain[0], frames, seq_len, heads_dev)
     keys = head_norm(proj[1], qk_gain[1], frames, seq_len, heads_dev)

time: 722 us -> 665 us (0.921)
  waiting for transfers between devices: 664 us -> 599 us
    all_gather x1 -> x0, waiting for transfers between devices: 398 us -> none  [on_device(): lax.all_gather(w_qkv, 'tm', axis=1, tiled=True)]
    ppermute x0 -> x3, waiting for transfers between devices: none -> 345 us  [the longest x1 186 us: summed_both_ways(): from_right = lax.ppermute(from_right, axis, behind)]
    all_gather x1, waiting for transfers between devices: 125 us -> 0.02 us  [on_device(): out_full = lax.all_gather(w_out, 'tm', axis=0, tiled=True)]
    unnamed x6 -> x5, waiting for transfers between devices: 33.6 us -> 150 us
    dot_general x1 -> x4, matrix products: 9.97 us -> 15 us  [on_device(): jnp.einsum('rd,cdh->crh', lax.dynamic_slice_in_dim(flat, at, shard.shape[...]
  transfers between devices with their start and end apart: 7 -> 9, of which waited for: 7 -> 7; matrix products, arithmetic and copies ran while one was open for 3% -> 4% of each run, Pallas kernels for 0% -> 0%
where the time goes in v1:
time: 665 us
  waiting for transfers between devices  599 us (90%)
  matrix products  26.8 us (4%)
  between operations  14.2 us (2%)
  other arithmetic  12 us (2%)
  local copies, waits for them, and re-layouts  6.9 us (1%)
    ppermute x1, waiting for transfers between devices, summed_both_ways(): from_right = lax.ppermute(from_right, axis, behind)  186 us
    ppermute x2, waiting for transfers between devices, summed_both_ways(): from_left = lax.ppermute(from_left, axis, ahead)  158 us
    unnamed x5, waiting for transfers between devices  150 us
    ppermute x2, waiting for transfers between devices, from_behind(): return lax.ppermute(block, axis, route)  48.2 us
    reduce_scatter x1, waiting for transfers between devices, on_device(): lax.psum_scatter(jnp.concatenate(pieces, axis=0), ('seq', 'mp'), scatter_...  33.1 us
    all_gather x1, waiting for transfers between devices, on_device(): whole = lax.all_gather(hidden, 'seq', axis=1, tiled=True)  23.2 us
    dot_general x4, matrix products, on_device(): jnp.einsum('rd,cdh->crh', lax.dynamic_slice_in_dim(flat, at, shard.shape[...  15 us
  transfers between devices with their start and end apart: 9, of which 7 were waited for; matrix products, arithmetic and copies ran while one was open for 4% of the time, Pallas kernels for 0%

profile of v1, /device:TPU:25, one launch (start us, length us, event | category | flops | bytes accessed | tf_op | source)
XLA Modules:
  0.0 664.8 jit_solution(16927126989954970895)
XLA Ops:
  10.8 148.8 %all-reduce.3.cloned.1.call-done = f32[4,15360]{1,0:T(4,128)} async-done(((f32[4,15360]{1,0:T(4,128)}), f32[4,15360]{1,0:T(4,128)}) %all-reduce.3.cloned.1.call-update) | async-done | bytes 245776
  159.6 1.7 dynamic-slice_add_fusion
  164.5 2.1 collective-permute-start.2
  166.7 23.2 %all-gather.3.cloned.1.call-done = bf16[1,128,5120]{2,1,0:T(8,128)(2,1)} async-done(((bf16[1,64,5120]{2,1,0:T(8,128)(2,1)}), bf16[1,128,5120]{2,1,0:T(8,128)(2,1)}) %all-gather.3.cloned.1.call-update) | async-done | bytes 1310736 | tf_op jit(solution)/shard_map/all_gather | solution.py:104
  189.8 3.8 fusion.20
  193.7 186.4 %collective-permute-done = bf16[3,1280,768]{2,1,0:T(8,128)(2,1)} collective-permute-done((bf16[3,1280,768]{2,1,0:T(8,128)(2,1)}, bf16[3,1280,768]{2,1,0:T(8,128)(2,1)}, u32[]{:S(2)}, u32[]{:S(2)}) %collective-permute-start) | collective-permute-done | bytes 5898272 | tf_op jit(solution)/shard_map/ppermute | solution.py:23
  380.0 3.8 convolution_add_fusion.2
  383.8 3.7 convolution_add_fusion.1
  387.5 158.5 %collective-permute-done.2 = bf16[3,1280,768]{2,1,0:T(8,128)(2,1)} collective-permute-done((bf16[3,1280,768]{2,1,0:T(8,128)(2,1)}, bf16[3,1280,768]{2,1,0:T(8,128)(2,1)}, u32[]{:S(2)}, u32[]{:S(2)}) %collective-permute-start.2) | collective-permute-done | bytes 5898272 | tf_op jit(solution)/shard_map/ppermute | solution.py:21
  546.0 3.7 fusion.10
  554.9 3.6 fusion.2
  558.5 3.6 fusion.4
  562.1 1.3 fusion.6
  563.4 1.5 fusion
  564.8 1.7 pad_maximum_fusion
  567.7 1.6 dynamic-slice_reduce_fusion
  569.3 33.1 %reduce-scatter.2.cloned.1.call-done = f32[64,2560]{1,0:T(8,128)} async-done(((f32[256,2560]{1,0:T(8,128)}), f32[64,2560]{1,0:T(8,128)}) %reduce-scatter.2.cloned.1.call-update) | async-done | bytes 655376 | tf_op jit(solution)/shard_map/reduce_scatter | solution.py:139
  602.4 1.8 multiply_multiply_fusion
  604.2 1.3 collective-permute-start.3
  605.5 16.0 %collective-permute-done.3 = f32[64,2560]{1,0:T(8,128)S(1)} collective-permute-done((f32[64,2560]{1,0:T(8,128)S(1)}, f32[64,2560]{1,0:T(8,128)S(1)}, u32[]{:S(2)}, u32[]{:S(2)}) %collective-permute-start.3) | collective-permute-done | bytes 655392 | tf_op jit(solution)/shard_map/ppermute | solution.py:32
  621.5 1.7 fusion.50
  623.3 1.3 collective-permute-start.4
  624.6 32.2 %collective-permute-done.4 = f32[64,2560]{1,0:T(8,128)S(1)} collective-permute-done((f32[64,2560]{1,0:T(8,128)S(1)}, f32[64,2560]{1,0:T(8,128)S(1)}, u32[]{:S(2)}, u32[]{:S(2)}) %collective-permute-start.4) | collective-permute-done | bytes 655392 | tf_op jit(solution)/shard_map/ppermute | solution.py:32
  656.7 1.5 fusion.16
  (53 shorter events, 12.9 us)
Async XLA Ops:
  6.5 1.8 copy-start
  6.5 3.6 copy-start.7
  6.5 3.0 copy-start.2
  6.5 153.1 %all-reduce.3.cloned.1.call-start = ((), (), s32[]{:S(2)}) async-start(), calls=%async_computation.4 | async-start | bytes 491520
  9.5 180.4 %all-gather.3.cloned.1.call-start = ((), (), s32[]{:S(2)}) async-start(), calls=%async_computation.1 | async-start | bytes 1966080 | tf_op jit(solution)/shard_map/all_gather | solution.py:104
  9.5 155.0 %collective-permute-start.1 = (bf16[3,1280,768]{2,1,0:T(8,128)(2,1)}, bf16[3,1280,768]{2,1,0:T(8,128)(2,1)}, u32[]{:S(2)}, u32[]{:S(2)}) collective-permute-start(bf16[3,1280,768]{2,1,0:T(8,128)(2,1)} %param.8), channel_id=1, source_target_pairs={{0,4},{4,8},{8,12},{12,0},{1,5},{5,9},{9,13},{13,1},{2,6},{6,10},{... | collective-permute-start | bytes 17694728 | tf_op jit(solution)/shard_map/ppermute | solution.py:21
  161.3 5.3 copy-start.5
  162.5 392.4 %all-gather.5.cloned.1.call-start = ((), (), s32[]{:S(2)}) async-start(), calls=%async_computation.2 | async-start | bytes 9830400 | tf_op jit(solution)/shard_map/all_gather | solution.py:124
  163.3 439.2 %reduce-scatter.2.cloned.1.call-start = ((), (), s32[]{:S(2)}) async-start(), calls=%async_computation.3 | async-start | bytes 3276800 | tf_op jit(solution)/shard_map/reduce_scatter | solution.py:139
  163.3 216.7 %collective-permute-start = (bf16[3,1280,768]{2,1,0:T(8,128)(2,1)}, bf16[3,1280,768]{2,1,0:T(8,128)(2,1)}, u32[]{:S(2)}, u32[]{:S(2)}) collective-permute-start(bf16[3,1280,768]{2,1,0:T(8,128)(2,1)} %param.8), channel_id=1, source_target_pairs={{0,12},{4,0},{8,4},{12,8},{1,13},{5,1},{9,5},{13,9},{2,14},{6,2},{... | collective-permute-start | bytes 17694728 | tf_op jit(solution)/shard_map/ppermute | solution.py:23
  164.5 381.5 %collective-permute-start.2 = (bf16[3,1280,768]{2,1,0:T(8,128)(2,1)}, bf16[3,1280,768]{2,1,0:T(8,128)(2,1)}, u32[]{:S(2)}, u32[]{:S(2)}) collective-permute-start(bf16[3,1280,768]{2,1,0:T(8,128)(2,1)} %collective-permute-done.1), channel_id=1, source_target_pairs={{0,4},{4,8},{8,12},{12,0},{1,5},{5,9},{9,13},{13,1},{2,6},{6,10},{... | collective-permute-start | bytes 17694728 | tf_op jit(solution)/shard_map/ppermute | solution.py:21
  189.8 190.2 %copy-start.4 = (bf16[1,128,5120]{2,1,0:T(8,128)(2,1)S(1)}, bf16[1,128,5120]{2,1,0:T(8,128)(2,1)}, u32[]{:S(2)}) copy-start(bf16[1,128,5120]{2,1,0:T(8,128)(2,1)} %all-gather.3.cloned.1.call-done) | copy-start | bytes 3932164
  554.9 7.2 %copy-start.1 = (bf16[5120,768]{1,0:T(8,128)(2,1)S(1)}, bf16[5120,768]{1,0:T(8,128)(2,1)}, u32[]{:S(2)}) copy-start(bf16[5120,768]{1,0:T(8,128)(2,1)} %all-gather.5.cloned.1.call-done) | copy-start | bytes 23592964
  566.5 0.6 copy-start.6
  602.4 54.3 %copy-start.3 = (f32[64,2560]{1,0:T(8,128)S(1)}, f32[64,2560]{1,0:T(8,128)}, u32[]{:S(2)}) copy-start(f32[64,2560]{1,0:T(8,128)} %reduce-scatter.2.cloned.1.call-done) | copy-start | bytes 1966084
  604.2 17.3 %collective-permute-start.3 = (f32[64,2560]{1,0:T(8,128)S(1)}, f32[64,2560]{1,0:T(8,128)S(1)}, u32[]{:S(2)}, u32[]{:S(2)}) collective-permute-start(f32[64,2560]{1,0:T(8,128)S(1)} %multiply_multiply_fusion), channel_id=1, source_target_pairs={{0,4},{4,8},{8,12},{1,5},{5,9},{9,13},{2,6},{6,10},{10,14},{3,7},{... | collective-permute-start | bytes 1966088 | tf_op jit(solution)/shard_map/ppermute | solution.py:32
  623.3 33.5 %collective-permute-start.4 = (f32[64,2560]{1,0:T(8,128)S(1)}, f32[64,2560]{1,0:T(8,128)S(1)}, u32[]{:S(2)}, u32[]{:S(2)}) collective-permute-start(f32[64,2560]{1,0:T(8,128)S(1)} %fusion.50), channel_id=1, source_target_pairs={{0,8},{4,12},{1,9},{5,13},{2,10},{6,14},{3,11},{7,15},{16,24},{20,... | collective-permute-start | bytes 1966088 | tf_op jit(solution)/shard_map/ppermute | solution.py:32
Sparse Core Ops, SparseCore 0:
  9.7 149.8 all-reduce.2
  162.6 27.1 all-gather.2
  191.4 293.0 all-gather.4
  566.7 35.6 reduce-scatter.1
